TPU v7x, 128 devices: a whole 4x4x4 slice. The times are simulated.
128 devices in a mesh: blk: 32 (over x, y, core), mp: 4 (over z).
Axes of the slice: x: 4, y: 4, z: 4, core: 2. Of those that a mesh axis runs over, the one named last changes fastest.
Arguments:
- hidden: bfloat16 [144, 3584], replicated, may hold values from -6 to 6
- medusa_w: bfloat16 [2, 3584, 3584], P(None, 'blk', 'mp'), may hold values from -0.09375 to 0.09375
- embedding: bfloat16 [131072, 3584], P(('blk', 'mp')), may hold values from -0.5 to 0.5
- cand_ids: int32 [2, 144, 10], replicated, may hold values from 0 to 131071
- tree_q: bfloat16 [12, 48, 4096], P(None, None, 'mp'), may hold values from -6 to 6
- tree_key_value: bfloat16 [2, 12, 48, 2048], P(None, None, None, 'mp'), may hold values from -6 to 6
- prompt_key_value: bfloat16 [2, 32, 2048, 2048], P(None, 'blk', None, 'mp'), may hold values from -6 to 6
- block_group: int32 [32], P('blk'), may hold values from 0 to 11, as said below
- block_len: int32 [32], P('blk'), may hold values from 1 to 2048
- block_empty: int32 [32], P('blk'), may hold values 0 or 1
- parents: int32 [12, 48], replicated, may hold values from 0 to 46, as said below
- out_weight: bfloat16 [4096, 3584], P('mp'), may hold values from -0.09375 to 0.09375
- post_gain: float32 [3584], replicated, may hold values from 0.5 to 1.5
- resid: bfloat16 [576, 3584], P('blk'), may hold values from -6 to 6
Outputs:
- draft_logprob: float32 [2, 144, 10], replicated
- layer_out: bfloat16 [576, 3584], P('blk')
Inputs may be any that keep to these rules, and one draw needn't show every extreme that they name: `block_group`: every group number from 0 to min(12, 32) - 1 owns at least one block. `parents`: entry 0 of each row is 0; entry i for i >= 1 is below i; some group's last token has parent 48 - 2.
All inputs are finite; a program needn't handle non-finite values. No bound on the sum of `block_empty` on one device may be relied on, other than what follows from the above.
Results may differ from a plain program's by a relative error of at most 0.005.
Values may be sent and summed in bfloat16 or wider, within the bound.
A program may use at most 128 MiB of HBM per device.

v0:
```python
import jax
import jax.numpy as jnp
from jax import lax
from jax.sharding import PartitionSpec as P

HEAD_SIZE = 256


def capped(values, limit):
    return limit * jnp.tanh(values / limit)


def ancestry(parents):
    count = parents.shape[1]
    column = jnp.arange(count, dtype=jnp.int32)
    linked = (parents[:, :, None] == column[None, None, :]) & (column[None, :, None] > 0)
    reach = jnp.eye(count, dtype=jnp.float32)[None] + linked.astype(jnp.float32)
    for sweep in range(count.bit_length()):
        reach = jnp.minimum(
            jnp.einsum("gij,gjk->gik", reach, reach, precision=lax.Precision.HIGHEST), 1.0
        )
    return reach


def attend(queries, keys, values, mask):
    rows = queries.shape[0]
    length = keys.shape[0]
    kv_heads = keys.shape[1] // HEAD_SIZE
    repeats = queries.shape[1] // keys.shape[1]
    query_view = queries.reshape(rows, kv_heads, repeats, HEAD_SIZE)
    key_view = keys.reshape(length, kv_heads, HEAD_SIZE)
    value_view = values.reshape(length, kv_heads, HEAD_SIZE)
    scores = jnp.einsum(
        "qhrd,khd->hrqk", query_view, key_view, preferred_element_type=jnp.float32
    ) * HEAD_SIZE ** (-0.5)
    weights = jnp.exp(capped(scores, 50.0)) * mask[None, None]
    denominator = jnp.sum(weights, -1).transpose(2, 0, 1).reshape(rows, kv_heads * repeats)
    numerator = jnp.einsum(
        "hrqk,khd->qhrd",
        weights.astype(jnp.bfloat16),
        value_view,
        preferred_element_type=jnp.float32,
    )
    return (numerator.reshape(rows, kv_heads * repeats * HEAD_SIZE), denominator)


def per_device(
    hidden,
    medusa_w,
    embedding,
    cand_ids,
    tree_q,
    tree_key_value,
    prompt_key_value,
    block_group,
    block_len,
    block_empty,
    parents,
    out_weight,
    post_gain,
    resid,
):
    units = medusa_w.shape[2]
    inner = jnp.einsum(
        "rd,mdu->mru",
        hidden,
        lax.all_gather(medusa_w, "blk", axis=1, tiled=True),
        preferred_element_type=jnp.float32,
    )
    own_cols = lax.dynamic_slice_in_dim(hidden, lax.axis_index("mp") * units, units, 1).astype(
        jnp.float32
    )
    fresh = (own_cols[None] + jax.nn.silu(inner)).astype(jnp.bfloat16)
    full_fresh = lax.all_gather(fresh, "mp", axis=2, tiled=True)
    logits = capped(
        jnp.einsum("mrd,vd->mrv", full_fresh, embedding, preferred_element_type=jnp.float32), 30.0
    )
    totals = jnp.sum(jnp.exp(logits), -1)
    vocab_dev = embedding.shape[0]
    first_id = lax.axis_index(("blk", "mp")) * vocab_dev
    local_ids = cand_ids - first_id
    match = local_ids[..., None] == jnp.arange(vocab_dev, dtype=jnp.int32)
    picked = jnp.sum(jnp.where(match, logits[:, :, None, :], 0.0), -1)
    totals, picked = lax.psum((totals, picked), ("blk", "mp"))
    draft_logprob = picked - jnp.log(totals)[..., None]
    groups, tree_size, features = tree_q.shape
    keys = prompt_key_value[0, 0]
    values = prompt_key_value[1, 0]
    length = keys.shape[0]
    group = block_group[0]
    key_ok = ((jnp.arange(length, dtype=jnp.int32) < block_len[0]) & (block_empty[0] == 0)).astype(
        jnp.float32
    )
    row_group = jnp.arange(groups * tree_size, dtype=jnp.int32) // tree_size
    mask = (row_group == group).astype(jnp.float32)[:, None] * key_ok[None, :]
    numer, denom = attend(tree_q.reshape(groups * tree_size, features), keys, values, mask)
    rows_dev = groups * tree_size // lax.axis_size("blk")
    first_row = lax.axis_index("blk") * rows_dev
    summed = lax.psum((numer, denom), "blk")
    numer = lax.dynamic_slice_in_dim(summed[0], first_row, rows_dev, 0)
    denom = lax.dynamic_slice_in_dim(summed[1], first_row, rows_dev, 0)
    reach = ancestry(parents)
    tree_numer, tree_denom = jax.vmap(attend)(tree_q, tree_key_value[0], tree_key_value[1], reach)
    heads_dev = tree_denom.shape[2]
    tree_numer = lax.dynamic_slice_in_dim(
        tree_numer.reshape(groups * tree_size, features), first_row, rows_dev, 0
    )
    tree_denom = lax.dynamic_slice_in_dim(
        tree_denom.reshape(groups * tree_size, heads_dev), first_row, rows_dev, 0
    )
    numer = numer + tree_numer
    denom = denom + tree_denom
    heads_out = (
        (numer.reshape(rows_dev, heads_dev, HEAD_SIZE) / denom[..., None])
        .reshape(rows_dev, features)
        .astype(jnp.bfloat16)
    )
    attn = lax.psum(jnp.dot(heads_out, out_weight, preferred_element_type=jnp.float32), "mp")
    normed = attn * lax.rsqrt(jnp.mean(attn * attn, -1, keepdims=True) + 1e-06) * post_gain
    layer_out = (normed + resid.astype(jnp.float32)).astype(jnp.bfloat16)
    return (draft_logprob, layer_out)


def solution(mesh):
    placed = (
        P(),
        P(None, "blk", "mp"),
        P(("blk", "mp"), None),
        P(),
        P(None, None, "mp"),
        P(None, None, None, "mp"),
        P(None, "blk", None, "mp"),
        P("blk"),
        P("blk"),
        P("blk"),
        P(),
        P("mp", None),
        P(),
        P("blk", None),
    )
    return jax.shard_map(
        per_device, mesh=mesh, in_specs=placed, out_specs=(P(), P("blk", None)), check_vma=False
    )
```

profile of v0, /device:TPU:1, one launch (start us, length us, event | category | flops | bytes accessed | tf_op | source)
XLA Modules:
  0.0 381.7 jit_solution(4261685247920140671)
XLA Ops:
  7.2 0.0 all-reduce.4.cloned.1.call-start
  7.2 4.4 %fusion.51 = (bf16[1,1,2048,512]{3,2,1,0:T(8,128)(2,1)}, bf16[1,1,2048,512]{3,2,1,0:T(8,128)(2,1)}) fusion(bf16[2,1,2048,512]{3,2,1,0:T(8,128)(2,1)} %param.20), kind=kLoop, calls=%fused_computation.70 | loop fusion | bytes 8388608 | tf_op jit(solution)/shard_map/slice | solution.py:88
  11.6 2.9 copy.79
  16.5 3.3 reshape_reshape.3
  19.8 4.0 %copy.80 = bf16[1,1,2048,512]{2,3,1,0:T(8,128)(2,1)} copy(bf16[1,1,2048,512]{3,2,1,0:T(8,128)(2,1)} %get-tuple-element.6) | data formatting | bytes 4194304
  23.8 0.4 broadcast_multiply_fusion
  24.2 10.5 %fusion = (f32[2,2,576]{2,1,0:T(2,128)}, f32[2,2048,576,2]{1,2,3,0:T(8,128)}) fusion(f32[576,2048]{1,0:T(8,128)S(1)} %broadcast_multiply_fusion, bf16[2048,2,256,1]{0,2,3,1:T(8,128)(2,1)S(1)} %bitcast.83, bf16[576,2,2,256]{3,2,1,0:T(2,128)(2,1)S(1)} %reshape_reshape.3), kind=kOutput, calls=%fused_computation.1 | convolution fusion | flops 2434791168 | bytes 26878976 | tf_op jit(solution)/shard_map/qhrd,khd->hrqk/dot_general | solution.py:33
  34.7 9.1 %fusion.6 = f32[576,2,2,256]{3,0,2,1:T(8,128)S(1)} fusion(bf16[2048,2,256,1]{0,2,3,1:T(8,128)(2,1)S(1)} %bitcast.85, f32[2,2048,576,2]{1,2,3,0:T(8,128)} %get-tuple-element.15, f32[576,2048]{1,0:T(8,128)S(1)} %broadcast_multiply_fusion), kind=kOutput, calls=%fused_computation.10 | convolution fusion | flops 2434793472 | bytes 28049408 | tf_op jit(solution)/shard_map/hrqk,khd->qhrd/dot_general | solution.py:38
  43.8 1.8 copy.56
  45.6 2.9 reshape.101
  48.6 0.0 all-gather.3.cloned.1.call-start
  48.6 0.7 all-gather.3.cloned.1.call-update
  49.3 0.2 all-reduce.6.cloned.1.call-start
  49.6 0.3 copy-done
  49.8 0.9 reshape.102
  50.7 0.7 reshape.104
  51.4 0.1 fusion.52
  51.5 0.1 reshape_squeeze.14
  51.7 1.4 convolution_minimum_fusion.5
  53.1 0.4 convolution_minimum_fusion.4
  53.5 0.4 convolution_minimum_fusion.3
  53.9 0.4 convolution_minimum_fusion.2
  54.4 0.4 convolution_minimum_fusion.1
  54.8 0.4 convolution_minimum_fusion
  55.2 0.1 copy.59
  55.3 0.9 fusion.53
  56.2 0.1 reshape.105
  56.3 124.9 %psum.38 = f32[576,4]{0,1:T(4,128)S(1)} all-reduce(f32[576,4]{0,1:T(4,128)S(1)} %reshape.104), channel_id=1, replica_groups=mesh['blk'=32,'mp'=4] {'blk'}, use_global_device_ids=true, to_apply=%region_6.7 | all-reduce | flops 2304 | bytes 18432 | tf_op jit(solution)/shard_map/psum | solution.py:99
  181.2 0.1 dynamic-slice_add_fusion
  181.3 0.1 copy.64
  181.4 0.1 div.48
  181.5 0.1 reshape_squeeze.15
  181.7 0.5 convolution_bitcast_fusion
  182.2 1.8 copy.62
  184.1 2.9 reshape.103
  187.0 0.0 all-reduce.4.cloned.1.call-done
  187.1 5.1 %fusion.39 = f32[18,3584]{1,0:T(8,128)} fusion(bf16[1024,3584]{1,0:T(8,128)(2,1)} %param.25, f32[18,1024]{1,0:T(8,128)S(1)} %bitcast.87, f32[576,1024]{1,0:T(8,128)} %reshape.103, s32[]{:T(128)S(6)} %select_n.25, f32[576,1024]{1,0:T(8,128)} %all-reduce.4.cloned.1.call-done), kind=kOutput, calls=%fused_computation.47 | convolution fusion | flops 132175872 | bytes 7868420 | tf_op jit(solution)/shard_map/dot_general | solution.py:118
  192.2 0.3 all-gather.5.cloned.1.call-start
  192.4 32.7 %all-gather.3.cloned.1.call-done = bf16[2,3584,896]{2,1,0:T(8,128)(2,1)} async-done(((bf16[2,112,896]{2,1,0:T(8,128)(2,1)}), bf16[2,3584,896]{2,1,0:T(8,128)(2,1)}) %all-gather.3.cloned.1.call-update) | async-done | bytes 12845072 | tf_op jit(solution)/shard_map/all_gather | solution.py:67
  225.2 7.6 %add_convert_fusion = bf16[2,144,896]{2,1,0:T(8,128)(2,1)} fusion(bf16[2,3584,896]{2,1,0:T(8,128)(2,1)} %all-gather.3.cloned.1.call-done, bf16[144,3584]{1,0:T(8,128)(2,1)S(1)} %copy-done.4, f32[144,896]{1,0:T(8,128)S(1)} %dynamic-slice_convert_fusion), kind=kOutput, calls=%fused_computation.32 | convolution fusion | flops 1851236352 | bytes 14909440 | tf_op jit(solution)/shard_map/rd,mdu->mru/dot_general | solution.py:64
  232.8 34.1 %all-reduce.6.cloned.1.call-done = f32[18,3584]{1,0:T(8,128)} async-done(((f32[18,3584]{1,0:T(8,128)}), f32[18,3584]{1,0:T(8,128)}) %all-reduce.6.cloned.1.call-update) | async-done | bytes 258064 | tf_op jit(solution)/shard_map/psum | solution.py:118
  266.9 1.1 multiply_reduce_fusion
  268.0 1.8 add_convert_fusion.1
  269.8 31.7 %all-gather.5.cloned.1.call-done = bf16[2,144,3584]{2,1,0:T(8,128)(2,1)} async-done(((bf16[2,144,896]{2,1,0:T(8,128)(2,1)}), bf16[2,144,3584]{2,1,0:T(8,128)(2,1)}) %all-gather.5.cloned.1.call-update) | async-done | bytes 2064400 | tf_op jit(solution)/shard_map/all_gather | solution.py:74
  301.5 6.2 %exponential_reduce_fusion = (f32[2,144]{1,0:T(2,128)S(1)}, f32[2,144,1024]{2,1,0:T(8,128)S(1)}) fusion(bf16[2,144,3584]{2,1,0:T(8,128)(2,1)} %all-gather.5.cloned.1.call-done, bf16[1024,3584]{1,0:T(8,128)(2,1)} %param.16), kind=kOutput, calls=%fused_computation.24 | convolution fusion | flops 2114813696 | bytes 10585216 | tf_op jit(solution)/shard_map/mrd,vd->mrv/dot_general | solution.py:76
  307.8 1.8 select_reduce_fusion
  309.6 64.9 %all-reduce = (f32[2,144,10]{1,2,0:T(8,128)S(1)}, f32[2,144]{1,0:T(2,128)S(1)}) all-reduce(f32[2,144,10]{1,2,0:T(8,128)S(1)} %select_reduce_fusion, f32[2,144]{1,0:T(2,128)S(1)} %get-tuple-element.10), channel_id=1, replica_groups=mesh['blk'=32,'mp'=4] {'blk','mp'}, use_global_device_ids=true, to_apply=%region_1.2 | all-reduce | flops 3168 | bytes 25344 | tf_op jit(solution)/shard_map/psum | solution.py:84
  374.5 0.6 copy.65
  (29 shorter events, 0.2 us)
Async XLA Ops:
  7.2 179.9 %all-reduce.4.cloned.1.call-start = ((), (), s32[]{:S(2)}) async-start(), calls=%async_computation.2 | async-start | bytes 4718592 | tf_op jit(solution)/shard_map/psum | solution.py:99
  24.2 10.5 %copy-start.1 = (bf16[1,1,2048,512]{2,3,1,0:T(8,128)(2,1)S(1)}, bf16[1,1,2048,512]{2,3,1,0:T(8,128)(2,1)}, u32[]{:S(2)}) copy-start(bf16[1,1,2048,512]{2,3,1,0:T(8,128)(2,1)} %copy.80) | copy-start | bytes 6291460
  48.6 1.3 copy-start
  48.6 2.9 copy-start.2
  48.6 176.6 %all-gather.3.cloned.1.call-start = ((), (), s32[]{:S(2)}) async-start(), calls=%async_computation | async-start | bytes 13246464 | tf_op jit(solution)/shard_map/all_gather | solution.py:67
  49.3 217.6 %all-reduce.6.cloned.1.call-start = ((), (), s32[]{:S(2)}) async-start(), calls=%async_computation.3 | async-start | bytes 688128 | tf_op jit(solution)/shard_map/psum | solution.py:118
  184.0 3.0 copy-start.4
  192.1 40.7 %copy-start.5 = (s32[2,144,10]{1,0,2:T(2,128)S(1)}, s32[2,144,10]{1,0,2:T(2,128)}, u32[]{:S(2)}) copy-start(s32[2,144,10]{1,0,2:T(2,128)} %param.17) | copy-start | bytes 34564
  192.2 75.9 %copy-start.3 = (bf16[18,3584]{1,0:T(8,128)(2,1)S(1)}, bf16[18,3584]{1,0:T(8,128)(2,1)}, u32[]{:S(2)}) copy-start(bf16[18,3584]{1,0:T(8,128)(2,1)} %param.27) | copy-start | bytes 387076
  192.2 75.9 %copy-start.6 = (f32[3584]{0:T(1024)S(1)}, f32[3584]{0:T(1024)}, u32[]{:S(2)}) copy-start(f32[3584]{0:T(1024)} %param.26) | copy-start | bytes 43012
  192.2 109.4 %all-gather.5.cloned.1.call-start = ((), (), s32[]{:S(2)}) async-start(), calls=%async_computation.1 | async-start | bytes 2580480 | tf_op jit(solution)/shard_map/all_gather | solution.py:74
Sparse Core Ops, SparseCore 0:
  48.7 110.4 all-reduce.3
  161.6 63.5 all-gather.2
  227.5 39.3 all-reduce.5
  268.4 33.0 all-gather.4
where the time goes:
time: 382 us
  blocking collectives  190 us (50%)
  waiting for transfers between devices  99.3 us (26%)
  matrix products  43.3 us (11%)
  local copies, waits for them, and re-layouts  27.5 us (7%)
  between operations  16 us (4%)
  other arithmetic  5.25 us (1%)
    psum x1, blocking collectives, per_device(): summed = lax.psum((numer, denom), 'blk')  125 us
    psum x1, blocking collectives, per_device(): totals, picked = lax.psum((totals, picked), ('blk', 'mp'))  64.9 us
    psum x1, waiting for transfers between devices, per_device(): lax.psum(jnp.dot(heads_out, out_weight, preferred_element_type=jnp.float3...  34.1 us
    all_gather x1, waiting for transfers between devices, per_device(): lax.all_gather(medusa_w, 'blk', axis=1, tiled=True)  32.7 us
    all_gather x1, waiting for transfers between devices, per_device(): full_fresh = lax.all_gather(fresh, 'mp', axis=2, tiled=True)  31.7 us
    dot_general x2, matrix products, attend(): jnp.einsum('qhrd,khd->hrqk', query_view, key_view, preferred_element_type...  11.3 us
    dot_general x2, matrix products, attend(): jnp.einsum('hrqk,khd->qhrd', weights.astype(jnp.bfloat16), value_view, pr...  9.63 us
    unnamed x19, local copies, waits for them, and re-layouts  7.84 us
  transfers between devices with their start and end apart: 4, of which 3 were waited for; matrix products, arithmetic and copies ran while one was open for 7% of the time, Pallas kernels for 0%

commit v1 on v0

--- a/solution.py
+++ b/solution.py
@@ -81,7 +81,7 @@
     local_ids = cand_ids - first_id
     match = local_ids[..., None] == jnp.arange(vocab_dev, dtype=jnp.int32)
     picked = jnp.sum(jnp.where(match, logits[:, :, None, :], 0.0), -1)
-    totals, picked = lax.psum((totals, picked), ("blk", "mp"))
+    totals, picked = lax.psum(lax.psum((totals, picked), "blk"), "mp")
     draft_logprob = picked - jnp.log(totals)[..., None]
     groups, tree_size, features = tree_q.shape
     keys = prompt_key_value[0, 0]

time: 382 us -> 328 us (0.86)
  blocking collectives: 190 us -> 136 us
  waiting for transfers between devices: 99.3 us -> 89.4 us
  other arithmetic: 5.25 us -> 9.69 us
    psum x2, blocking collectives: 190 us -> 136 us  [per_device(): totals, picked = lax.psum(lax.psum((totals, picked), 'blk'), 'mp')]
    all_gather x1, waiting for transfers between devices: 31.7 us -> 0.01 us  [per_device(): full_fresh = lax.all_gather(fresh, 'mp', axis=2, tiled=True)]
    all_gather x1, waiting for transfers between devices: 32.7 us -> 61.9 us  [per_device(): lax.all_gather(medusa_w, 'blk', axis=1, tiled=True)]
    psum x1, waiting for transfers between devices: 34.1 us -> 26.8 us  [per_device(): lax.psum(jnp.dot(heads_out, out_weight, preferred_element_type=jnp.float3...]
    unnamed x19 -> x23, local copies, waits for them, and re-layouts: 7.84 us -> 8.09 us
  transfers between devices with their start and end apart: 4 -> 4, of which waited for: 3 -> 2; matrix products, arithmetic and copies ran while one was open for 7% -> 21% of each run, Pallas kernels for 0% -> 0%
where the time goes in v1:
time: 328 us; the launch traced here: 326 us
  blocking collectives  136 us (41%)
  waiting for transfers between devices  89.4 us (27%)
  matrix products  45.2 us (14%)
  local copies, waits for them, and re-layouts  29.1 us (9%)
  between operations  16 us (5%)
  other arithmetic  9.69 us (3%)
    psum x2, blocking collectives, per_device(): totals, picked = lax.psum(lax.psum((totals, picked), 'blk'), 'mp')  136 us
    all_gather x1, waiting for transfers between devices, per_device(): lax.all_gather(medusa_w, 'blk', axis=1, tiled=True)  61.9 us
    psum x1, waiting for transfers between devices, per_device(): lax.psum(jnp.dot(heads_out, out_weight, preferred_element_type=jnp.float3...  26.8 us
    dot_general x2, matrix products, attend(): jnp.einsum('qhrd,khd->hrqk', query_view, key_view, preferred_element_type...  13.1 us
    dot_general x2, matrix products, attend(): jnp.einsum('hrqk,khd->qhrd', weights.astype(jnp.bfloat16), value_view, pr...  9.6 us
    unnamed x23, local copies, waits for them, and re-layouts  8.09 us
    dot_general x1, matrix products, per_device(): jnp.einsum('rd,mdu->mru', hidden, lax.all_gather(medusa_w, 'blk', axis=1,...  7.56 us
  transfers between devices with their start and end apart: 4, of which 2 were waited for; matrix products, arithmetic and copies ran while one was open for 21% of the time, Pallas kernels for 0%

profile of v1, /device:TPU:1, one launch (start us, length us, event | category | flops | bytes accessed | tf_op | source)
XLA Modules:
  0.0 325.6 jit_solution(3094606066992411119)
XLA Ops:
  7.2 0.7 all-gather.3.cloned.1.call-update
  9.9 1.0 dynamic-slice_convert_fusion
  10.9 4.5 %fusion.51 = (bf16[1,1,2048,512]{3,2,1,0:T(8,128)(2,1)}, bf16[1,1,2048,512]{3,2,1,0:T(8,128)(2,1)}) fusion(bf16[2,1,2048,512]{3,2,1,0:T(8,128)(2,1)} %param.20), kind=kLoop, calls=%fused_computation.70 | loop fusion | bytes 8388608 | tf_op jit(solution)/shard_map/slice | solution.py:88
  15.4 61.9 %all-gather.3.cloned.1.call-done = bf16[2,3584,896]{2,1,0:T(8,128)(2,1)} async-done(((bf16[2,112,896]{2,1,0:T(8,128)(2,1)}), bf16[2,3584,896]{2,1,0:T(8,128)(2,1)}) %all-gather.3.cloned.1.call-update) | async-done | bytes 12845072 | tf_op jit(solution)/shard_map/all_gather | solution.py:67
  77.3 7.6 %add_convert_fusion = bf16[2,144,896]{2,1,0:T(8,128)(2,1)} fusion(bf16[2,3584,896]{2,1,0:T(8,128)(2,1)} %all-gather.3.cloned.1.call-done, bf16[144,3584]{1,0:T(8,128)(2,1)S(1)} %copy-done.5, f32[144,896]{1,0:T(8,128)S(1)} %dynamic-slice_convert_fusion), kind=kOutput, calls=%fused_computation.32 | convolution fusion | flops 1851236352 | bytes 14909440 | tf_op jit(solution)/shard_map/rd,mdu->mru/dot_general | solution.py:64
  84.9 0.2 all-reduce.5.cloned.1.call-start
  85.1 2.5 broadcast_multiply_fusion
  87.6 2.9 copy.79
  90.6 4.0 %reshape_reshape.3 = bf16[576,2,2,256]{3,2,1,0:T(2,128)(2,1)} reshape(bf16[12,48,1024]{2,1,0:T(8,128)(2,1)} %param.18) | data formatting | bytes 2359296 | tf_op jit(solution)/shard_map/reshape;reshape | solution.py:30
  94.6 4.1 %copy.80 = bf16[1,1,2048,512]{2,3,1,0:T(8,128)(2,1)} copy(bf16[1,1,2048,512]{3,2,1,0:T(8,128)(2,1)} %get-tuple-element.9) | data formatting | bytes 4194304
  98.7 12.2 %fusion = (f32[2,2,576]{2,1,0:T(2,128)}, f32[2,2048,576,2]{1,2,3,0:T(8,128)}) fusion(f32[576,2048]{1,0:T(8,128)} %broadcast_multiply_fusion, bf16[2048,2,256,1]{0,2,3,1:T(8,128)(2,1)S(1)} %bitcast.85, bf16[576,2,2,256]{3,2,1,0:T(2,128)(2,1)} %reshape_reshape.3), kind=kOutput, calls=%fused_computation.1 | convolution fusion | flops 2434791168 | bytes 26878976 | tf_op jit(solution)/shard_map/qhrd,khd->hrqk/dot_general | solution.py:33
  110.9 9.1 %fusion.6 = f32[576,2,2,256]{3,0,2,1:T(8,128)S(1)} fusion(bf16[2048,2,256,1]{0,2,3,1:T(8,128)(2,1)S(1)} %bitcast.87, f32[2,2048,576,2]{1,2,3,0:T(8,128)} %get-tuple-element.16, f32[576,2048]{1,0:T(8,128)S(1)} %bitcast.84), kind=kOutput, calls=%fused_computation.10 | convolution fusion | flops 2434793472 | bytes 28049408 | tf_op jit(solution)/shard_map/hrqk,khd->qhrd/dot_general | solution.py:38
  120.0 1.8 copy.56
  121.8 2.9 reshape.101
  124.8 0.3 all-reduce.7.cloned.1.call-start
  125.0 0.6 fusion.40
  125.6 0.4 copy-done
  126.0 0.9 reshape.102
  126.9 0.7 broadcast_subtract_fusion.1
  127.7 0.6 copy.50
  128.3 0.7 reshape.104
  129.0 0.1 fusion.52
  129.1 0.1 reshape_squeeze.14
  129.2 1.4 convolution_minimum_fusion.5
  130.6 0.4 convolution_minimum_fusion.4
  131.1 0.4 convolution_minimum_fusion.3
  131.5 0.4 convolution_minimum_fusion.2
  131.9 0.4 convolution_minimum_fusion.1
  132.3 0.4 convolution_minimum_fusion
  132.8 0.1 copy.59
  132.9 0.9 fusion.53
  133.8 0.1 reshape.105
  133.9 0.1 reshape_squeeze.15
  134.0 0.5 convolution_bitcast_fusion
  134.6 1.8 copy.62
  136.4 2.9 reshape.103
  139.4 6.4 %exponential_reduce_fusion = (f32[2,144]{1,0:T(2,128)S(1)}, f32[2,144,1024]{2,1,0:T(8,128)S(1)}) fusion(bf16[2,144,3584]{2,1,0:T(8,128)(2,1)} %all-gather.5.cloned.1.call-done, bf16[1024,3584]{1,0:T(8,128)(2,1)} %param.16), kind=kOutput, calls=%fused_computation.24 | convolution fusion | flops 2114813696 | bytes 10585216 | tf_op jit(solution)/shard_map/mrd,vd->mrv/dot_general | solution.py:76
  145.7 1.8 select_reduce_fusion
  147.6 121.4 %all-reduce = (f32[2,144,10]{1,2,0:T(8,128)S(1)}, f32[2,144]{1,0:T(2,128)S(1)}, f32[576,4]{0,1:T(4,128)S(1)}) all-reduce(f32[2,144,10]{1,2,0:T(8,128)S(1)} %select_reduce_fusion, f32[2,144]{1,0:T(2,128)S(1)} %get-tuple-element.13, f32[576,4]{0,1:T(4,128)S(1)} %reshape.104), channel_id=1, replica_groups=mesh['blk'=32,'mp'=4] {'blk'}, use_global_device_ids=true, to_apply=%region_1.2 | all-reduce | flops 5472 | bytes 43776 | tf_op jit(solution)/shard_map/psum | solution.py:84
  269.0 0.1 dynamic-slice_add_fusion
  269.0 0.1 copy.64
  269.1 0.1 div.48
  269.3 5.1 %fusion.39 = f32[18,3584]{1,0:T(8,128)} fusion(bf16[1024,3584]{1,0:T(8,128)(2,1)} %param.25, f32[18,1024]{1,0:T(8,128)S(1)} %bitcast.89, f32[576,1024]{1,0:T(8,128)} %reshape.103, s32[]{:T(128)S(6)} %select_n.25, f32[576,1024]{1,0:T(8,128)} %all-reduce.5.cloned.1.call-done), kind=kOutput, calls=%fused_computation.47 | convolution fusion | flops 132175872 | bytes 7868420 | tf_op jit(solution)/shard_map/dot_general | solution.py:118
  274.5 14.2 %all-reduce.1 = (f32[2,144,10]{1,2,0:T(8,128)S(1)}, f32[2,144]{1,0:T(2,128)S(1)}) all-reduce(f32[2,144,10]{1,2,0:T(8,128)S(1)} %get-tuple-element.4, f32[2,144]{1,0:T(2,128)S(1)} %get-tuple-element.5), channel_id=1, replica_groups=mesh['blk'=32,'mp'=4] {'mp'}, use_global_device_ids=true, to_apply=%region_2.3 | all-reduce | flops 3168 | bytes 25344 | tf_op jit(solution)/shard_map/psum | solution.py:84
  288.7 0.6 copy.65
  289.4 26.8 %all-reduce.7.cloned.1.call-done = f32[18,3584]{1,0:T(8,128)} async-done(((f32[18,3584]{1,0:T(8,128)}), f32[18,3584]{1,0:T(8,128)}) %all-reduce.7.cloned.1.call-update) | async-done | bytes 258064 | tf_op jit(solution)/shard_map/psum | solution.py:118
  316.2 1.1 multiply_reduce_fusion
  317.3 1.8 add_convert_fusion.1
  (34 shorter events, 0.3 us)
Async XLA Ops:
  7.2 70.1 %all-gather.3.cloned.1.call-start = ((), (), s32[]{:S(2)}) async-start(), calls=%async_computation | async-start | bytes 13246464 | tf_op jit(solution)/shard_map/all_gather | solution.py:67
  7.9 131.5 %all-gather.5.cloned.1.call-start = ((), (), s32[]{:S(2)}) async-start(), calls=%async_computation.1 | async-start | bytes 2580480 | tf_op jit(solution)/shard_map/all_gather | solution.py:74
  10.9 66.4 %copy-start.5 = (bf16[144,3584]{1,0:T(8,128)(2,1)S(1)}, bf16[144,3584]{1,0:T(8,128)(2,1)}, u32[]{:S(2)}) copy-start(bf16[144,3584]{1,0:T(8,128)(2,1)} %param.14) | copy-start | bytes 3096580
  84.9 184.4 %all-reduce.5.cloned.1.call-start = ((), (), s32[]{:S(2)}) async-start(), calls=%async_computation.2 | async-start | bytes 4718592 | tf_op jit(solution)/shard_map/psum | solution.py:99
  94.6 16.3 %slice-start = ((s8[4718592]{0:T(1024)(128)(4,1)}), s8[524288]{0:T(1024)(128)(4,1)S(1)}, s32[]{:S(2)}) async-start(s8[4718592]{0:T(1024)(128)(4,1)} %bitcast.83), calls=%async_computation.4 | async-start | bytes 1048576
  98.7 12.2 %slice-start.1 = ((s8[4718592]{0:T(1024)(128)(4,1)}), s8[4194304]{0:T(1024)(128)(4,1)S(1)}, s32[]{:S(2)}) async-start(s8[4718592]{0:T(1024)(128)(4,1)} %bitcast.83), calls=%async_computation.5 | async-start | bytes 8388608
  98.7 12.2 %copy-start.1 = (bf16[1,1,2048,512]{2,3,1,0:T(8,128)(2,1)S(1)}, bf16[1,1,2048,512]{2,3,1,0:T(8,128)(2,1)}, u32[]{:S(2)}) copy-start(bf16[1,1,2048,512]{2,3,1,0:T(8,128)(2,1)} %copy.80) | copy-start | bytes 6291460
  124.7 1.3 copy-start
  124.7 4.3 %copy-start.2 = (bf16[2,12,48,512]{3,2,1,0:T(8,128)(2,1)S(1)}, bf16[2,12,48,512]{3,2,1,0:T(8,128)(2,1)}, u32[]{:S(2)}) copy-start(bf16[2,12,48,512]{3,2,1,0:T(8,128)(2,1)} %param.19) | copy-start | bytes 3538948
  124.8 191.4 %all-reduce.7.cloned.1.call-start = ((), (), s32[]{:S(2)}) async-start(), calls=%async_computation.3 | async-start | bytes 688128 | tf_op jit(solution)/shard_map/psum | solution.py:118
  139.3 6.4 %copy-start.4 = (s32[2,144,10]{1,2,0:T(8,128)S(1)}, s32[2,144,10]{1,2,0:T(8,128)}, u32[]{:S(2)}) copy-start(s32[2,144,10]{1,2,0:T(8,128)} %copy.50) | copy-start | bytes 34564
  269.3 48.0 %copy-start.3 = (bf16[18,3584]{1,0:T(8,128)(2,1)S(1)}, bf16[18,3584]{1,0:T(8,128)(2,1)}, u32[]{:S(2)}) copy-start(bf16[18,3584]{1,0:T(8,128)(2,1)} %param.27) | copy-start | bytes 387076
  269.3 48.0 %copy-start.6 = (f32[3584]{0:T(1024)S(1)}, f32[3584]{0:T(1024)}, u32[]{:S(2)}) copy-start(f32[3584]{0:T(1024)} %param.26) | copy-start | bytes 43012
Sparse Core Ops, SparseCore 0:
  10.4 66.8 all-gather.2
  85.0 29.9 all-gather.4
  124.9 106.3 all-reduce.4
  274.6 41.5 all-reduce.6
